TPU v7x, 512 devices: a whole 4x8x8 slice. The times are simulated.
512 devices in a mesh: dp: 8 (over z_lo, x), region: 64 (over y, z_hi, core).
Axes of the slice: x: 4, y: 8, z: 8 (z_hi: 4, z_lo: 2; z = z_hi * 2 + z_lo), core: 2. Of those that a mesh axis runs over, the one named last changes fastest.
Arguments:
- queries: bfloat16 [8, 8192, 1280], P('dp', 'region'), may hold values from -5 to 5
- keys: bfloat16 [8, 8192, 1280], P('dp', 'region'), may hold values from -5 to 5
- values: bfloat16 [8, 8192, 1280], P('dp', 'region'), may hold values from -6 to 6
- attn_out: bfloat16 [8, 8192, 1280], P('dp', 'region'), may hold values from -0.125 to 0.125
- d_out: bfloat16 [8, 8192, 2560], P('dp', 'region'), may hold values from -6 to 6
- w_out: bfloat16 [1280, 2560], P('dp'), may hold values from -0.15625 to 0.15625
- adjacency: int32 [64, 4, 12], P('region'), may hold values from 0 to 1, as said below
- counts: int32 [64], P('region'), may hold values from 1 to 4, as said below
Outputs:
- d_queries: bfloat16 [8, 8192, 1280], P('dp', 'region')
- d_keys: bfloat16 [8, 8192, 1280], P('dp', 'region')
- d_values: bfloat16 [8, 8192, 1280], P('dp', 'region')
- d_weight: bfloat16 [1280, 2560], P('dp')
Inputs may be any that keep to these rules, and one draw needn't show every extreme that they name: Region r has 4 token blocks, of which the first counts[r] are live; in some region all 4 are live. adjacency[r, a, j] = 1 lets query block a of region r see key block j % 4 of region (r + j // 4 - 1) mod 64; entry j = 4 + a is 1.
All inputs are finite; a program needn't handle non-finite values.
Results may differ from a plain program's by a relative error of at most 0.007.
Values may be sent and summed in bfloat16 or wider, within the bound.
No kernel may reach another device: no remote copies, remote signals or barrier semaphores. Data moves between devices by JAX's collectives and lax.ppermute only.
A program may use at most 64 MiB of HBM per device.

v0:
```python
import math
import jax
import jax.numpy as jnp
from jax import lax
from jax.sharding import PartitionSpec as P

HEADS = 8
HD = 160
BLK = 4


def from_behind(value, axis, by):
    length = lax.axis_size(axis)
    return lax.ppermute(value, axis, [(i, (i + by) % length) for i in range(length)])


def expand(blocks, block_rows):
    return jnp.repeat(jnp.repeat(blocks, block_rows, axis=0), block_rows, axis=1)


def score_block(query_rows, key_rows):
    scores = jnp.einsum("qhc,khc->hqk", query_rows, key_rows, preferred_element_type=jnp.float32)
    return scores * (1.0 / math.sqrt(HD))


def row_stats(scores, allowed):
    maxima = jnp.max(jnp.where(allowed[None], scores, -1e30), axis=2)
    totals = jnp.sum(jnp.exp(jnp.where(allowed[None], scores - maxima[:, :, None], -1e30)), axis=2)
    return (maxima, totals)


def backward_block(scores, allowed, lse, delta, query_rows, key_rows, value_rows, grad_rows):
    probs = jnp.exp(jnp.where(allowed[None], scores - lse[:, :, None], -1e30))
    probs_b = probs.astype(jnp.bfloat16)
    dvalue = jnp.einsum("hqk,qhc->khc", probs_b, grad_rows, preferred_element_type=jnp.float32)
    dprobs = jnp.einsum("qhc,khc->hqk", grad_rows, value_rows, preferred_element_type=jnp.float32)
    dscores = (probs * (dprobs - delta[:, :, None]) * (1.0 / math.sqrt(HD))).astype(jnp.bfloat16)
    dquery = jnp.einsum("hqk,khc->qhc", dscores, key_rows, preferred_element_type=jnp.float32)
    dkey = jnp.einsum("hqk,qhc->khc", dscores, query_rows, preferred_element_type=jnp.float32)
    return (dquery, dkey, dvalue)


def local(queries, keys, values, attn_out, d_out, w_out, adjacency, counts):
    tok_rows = queries.shape[1]
    block_rows = tok_rows // BLK
    width = queries.shape[2]
    live_blocks = jnp.arange(BLK) < counts[0]
    live_rows = jnp.repeat(live_blocks, block_rows)
    grads = d_out * live_rows[None, :, None].astype(jnp.bfloat16)
    gathered = lax.all_gather(grads, "dp", axis=1, tiled=True)
    out_cols = lax.all_to_all(attn_out, "dp", split_axis=2, concat_axis=1, tiled=True)
    attn_part = jnp.einsum("td,hd->th", gathered[0], w_out, preferred_element_type=jnp.float32)
    d_attn = lax.all_to_all(
        attn_part.astype(jnp.bfloat16)[None], "dp", split_axis=1, concat_axis=2, tiled=True
    )
    weight_part = jnp.einsum(
        "th,td->hd", out_cols[0], gathered[0], preferred_element_type=jnp.float32
    )
    d_weight = lax.psum(weight_part, "region").astype(jnp.bfloat16)
    query_rows = queries[0].reshape(tok_rows, HEADS, HD)
    out_rows = attn_out[0].reshape(tok_rows, HEADS, HD)
    grad_attn = d_attn[0].reshape(tok_rows, HEADS, HD)
    delta = jnp.einsum("qhc,qhc->hq", grad_attn, out_rows, preferred_element_type=jnp.float32)
    adjacent = adjacency[0] == 1
    own_block = jnp.arange(3 * BLK)[None, :] == BLK + jnp.arange(BLK)[:, None]
    key_live = live_rows.astype(jnp.bfloat16)
    fetched = {}
    for offset in (1, -1):
        fetched[offset] = from_behind((keys[0], values[0], key_live), "region", offset)
    key_window = jnp.concatenate([fetched[1][0], keys[0], fetched[-1][0]], 0).reshape(
        3 * tok_rows, HEADS, HD
    )
    value_window = jnp.concatenate([fetched[1][1], values[0], fetched[-1][1]], 0).reshape(
        3 * tok_rows, HEADS, HD
    )
    live_window = jnp.concatenate([fetched[1][2], key_live, fetched[-1][2]], 0)
    live_window = live_window.reshape(3 * BLK, block_rows)[:, 0] > 0.5
    allowed = expand(adjacent & live_window[None] | own_block, block_rows)
    scores = score_block(query_rows, key_window)
    maxima, totals = row_stats(scores, allowed)
    lse = maxima + jnp.log(totals)
    dquery, dkey_win, dvalue_win = backward_block(
        scores, allowed, lse, delta, query_rows, key_window, value_window, grad_attn
    )
    dkey = dkey_win[tok_rows : 2 * tok_rows]
    dvalue = dvalue_win[tok_rows : 2 * tok_rows]
    for offset, first in ((-1, 0), (1, 2)):
        lower = first * tok_rows
        returned = (
            from_behind(
                dkey_win[lower : lower + tok_rows].astype(jnp.bfloat16), "region", offset
            ).astype(jnp.float32),
            from_behind(
                dvalue_win[lower : lower + tok_rows].astype(jnp.bfloat16), "region", offset
            ).astype(jnp.float32),
        )
        dkey = dkey + returned[0]
        dvalue = dvalue + returned[1]
    out_shape = (1, tok_rows, width)
    return (
        dquery.astype(jnp.bfloat16).reshape(out_shape),
        dkey.astype(jnp.bfloat16).reshape(out_shape),
        dvalue.astype(jnp.bfloat16).reshape(out_shape),
        d_weight,
    )


def solution(mesh):
    return jax.shard_map(
        local,
        mesh=mesh,
        in_specs=(
            P("dp", "region", None),
            P("dp", "region", None),
            P("dp", "region", None),
            P("dp", "region", None),
            P("dp", "region", None),
            P("dp", None),
            P("region", None, None),
            P("region"),
        ),
        out_specs=(
            P("dp", "region", None),
            P("dp", "region", None),
            P("dp", "region", None),
            P("dp", None),
        ),
        check_vma=False,
    )
```

profile of v0, /device:TPU:2, one launch (start us, length us, event | category | flops | bytes accessed | tf_op | source)
XLA Modules:
  0.0 473.0 jit_solution(7799400725067004841)
XLA Ops:
  8.2 2.0 broadcast_multiply_fusion
  10.3 13.3 %collective-permute-start.3 = (bf16[128]{0:T(256)(128)(2,1)S(1)}, bf16[128]{0:T(256)(128)(2,1)S(1)}, u32[]{:S(2)}, u32[]{:S(2)}) collective-permute-start(bf16[128]{0:T(256)(128)(2,1)S(1)} %convert_element_type.56), channel_id=1, source_target_pairs={{0,63},{1,0},{2,1},{3,2},{4,3},{5,4},{6,5},{7,6},{8,7},{9,8},{10,9... | collective-permute-start | bytes 776 | tf_op jit(solution)/shard_map/ppermute | solution.py:14
  23.6 2.6 collective-permute-start.1
  26.1 1.9 collective-permute-start
  28.1 7.9 %collective-permute-start.5 = (bf16[128,1280]{1,0:T(8,128)(2,1)S(1)}, bf16[128,1280]{1,0:T(8,128)(2,1)}, u32[]{:S(2)}, u32[]{:S(2)}) collective-permute-start(bf16[128,1280]{1,0:T(8,128)(2,1)S(1)} %bitcast.121), channel_id=1, source_target_pairs={{0,63},{1,0},{2,1},{3,2},{4,3},{5,4},{6,5},{7,6},{8,7},{9,8},{10,9... | collective-permute-start | bytes 983048 | tf_op jit(solution)/shard_map/ppermute | solution.py:14
  36.0 1.9 collective-permute-start.4
  39.0 7.5 %reduce.5 = bf16[1280,128]{1,0:T(8,128)(2,1)S(1)} reduce(bf16[1280,1,128]{2,1,0:T(2,128)(2,1)S(1)} %bitcast.106, bf16[]{:T(256)} %broadcast.40), dimensions={1}, to_apply=%bitcast.90.reduce_sub_computation | reduce | bytes 655362
  47.3 5.9 %all-to-all-start.1 = ((bf16[8,2,10240]{2,1,0:T(2,128)(2,1)}), bf16[8,2,10240]{2,1,0:T(2,128)(2,1)S(1)}, u32[]{:S(2)}, u32[]{:S(2)}) async-start(bf16[8,2,10240]{2,1,0:T(2,128)(2,1)} %reshape.81), calls=%async_computation.1 | async-start | bytes 655360 | tf_op jit(solution)/shard_map/all_to_all | solution.py:51
  53.4 2.1 collective-permute-start.2
  57.7 4.8 %collective-permute-done.2 = bf16[128]{0:T(256)(128)(2,1)S(1)} collective-permute-done((bf16[128]{0:T(256)(128)(2,1)S(1)}, bf16[128]{0:T(256)(128)(2,1)S(1)}, u32[]{:S(2)}, u32[]{:S(2)}) %collective-permute-start.2) | collective-permute-done | bytes 288 | tf_op jit(solution)/shard_map/ppermute | solution.py:14
  63.3 1.3 copy.67
  64.7 2.0 copy.77
  66.7 1.9 copy.75
  69.3 1.2 copy-done.2
  71.8 20.1 %all-gather.2.cloned.1.call-done = bf16[1,1024,2560]{2,1,0:T(8,128)(2,1)} async-done(((bf16[1,128,2560]{2,1,0:T(8,128)(2,1)}), bf16[1,1024,2560]{2,1,0:T(8,128)(2,1)}) %all-gather.2.cloned.1.call-update) | async-done | bytes 5242896 | tf_op jit(solution)/shard_map/all_gather | solution.py:50
  92.0 3.6 fusion.4
  96.0 2.6 fusion.17
  98.6 2.4 copy.72
  100.9 4.9 %reduce.4 = bf16[1024,160]{1,0:T(8,128)(2,1)} reduce(bf16[1024,1,160]{2,1,0:T(2,128)(2,1)S(1)} %bitcast.104, bf16[]{:T(256)} %broadcast.40), dimensions={1}, to_apply=%bitcast.88.reduce_sub_computation | reduce | bytes 655362
  105.8 2.6 reshape.79
  108.4 10.2 %all-to-all-start = ((bf16[8,2,10240]{2,1,0:T(2,128)(2,1)}), bf16[8,2,10240]{2,1,0:T(2,128)(2,1)S(1)}, u32[]{:S(2)}, u32[]{:S(2)}) async-start(bf16[8,2,10240]{2,1,0:T(2,128)(2,1)} %reshape.79), calls=%async_computation | async-start | bytes 655360 | tf_op jit(solution)/shard_map/all_to_all | solution.py:53
  118.5 307.2 %all-reduce.1 = bf16[160,2560]{1,0:T(8,128)(2,1)} all-reduce(f32[160,2560]{1,0:T(8,128)S(1)} %fusion.4), channel_id=1, replica_groups=mesh['dp'=8,'region'=64] {'region'}, use_global_device_ids=true, to_apply=%region_2.3 | all-reduce | flops 409600 | bytes 2457600 | tf_op jit(solution)/shard_map/psum | solution.py:59
  425.7 2.1 reshape.80
  427.8 1.4 copy.104
  430.5 1.8 fusion.46
  433.2 2.1 collective-permute-start.8
  435.3 2.4 collective-permute-start.9
  440.2 7.6 %collective-permute-start.6 = (bf16[128,8,160]{0,2,1:T(8,128)(2,1)}, bf16[128,8,160]{0,2,1:T(8,128)(2,1)}, u32[]{:S(2)}, u32[]{:S(2)}) collective-permute-start(bf16[128,8,160]{0,2,1:T(8,128)(2,1)} %get-tuple-element.22), channel_id=1, source_target_pairs={{0,63},{1,0},{2,1},{3,2},{4,3},{5,4},{6,5},{7,6},{8,7},{9,8},{10,9... | collective-permute-start | bytes 983048 | tf_op jit(solution)/shard_map/ppermute | solution.py:14
  447.8 1.9 collective-permute-start.7
  451.8 1.4 fusion.30
  454.1 9.9 %collective-permute-done.7 = bf16[128,8,160]{0,2,1:T(8,128)(2,1)} collective-permute-done((bf16[128,8,160]{0,2,1:T(8,128)(2,1)S(1)}, bf16[128,8,160]{0,2,1:T(8,128)(2,1)}, u32[]{:S(2)}, u32[]{:S(2)}) %collective-permute-start.7) | collective-permute-done | bytes 327712 | tf_op jit(solution)/shard_map/ppermute | solution.py:14
  464.0 1.2 fusion.32
  (94 shorter events, 16.2 us)
Async XLA Ops:
  7.2 88.4 %copy-start = (bf16[160,2560]{1,0:T(8,128)(2,1)S(1)}, bf16[160,2560]{1,0:T(8,128)(2,1)}, u32[]{:S(2)}) copy-start(bf16[160,2560]{1,0:T(8,128)(2,1)} %param.13) | copy-start | bytes 2457604
  7.2 16.4 %copy-start.10 = (bf16[1,128,1280]{2,1,0:T(8,128)(2,1)S(1)}, bf16[1,128,1280]{2,1,0:T(8,128)(2,1)}, u32[]{:S(2)}) copy-start(bf16[1,128,1280]{2,1,0:T(8,128)(2,1)} %param.9) | copy-start | bytes 983044
  7.2 20.9 %copy-start.11 = (bf16[1,128,1280]{2,1,0:T(8,128)(2,1)S(1)}, bf16[1,128,1280]{2,1,0:T(8,128)(2,1)}, u32[]{:S(2)}) copy-start(bf16[1,128,1280]{2,1,0:T(8,128)(2,1)} %param.10) | copy-start | bytes 983044
  7.2 30.7 %copy-start.6 = (bf16[1,128,1280]{2,1,0:T(8,128)(2,1)S(1)}, bf16[1,128,1280]{2,1,0:T(8,128)(2,1)}, u32[]{:S(2)}) copy-start(bf16[1,128,1280]{2,1,0:T(8,128)(2,1)} %param.11) | copy-start | bytes 983044
  7.2 84.7 %all-gather.2.cloned.1.call-start = ((), (), s32[]{:S(2)}) async-start(), calls=%async_computation.2 | async-start | bytes 5898240 | tf_op jit(solution)/shard_map/all_gather | solution.py:50
  10.3 43.2 %collective-permute-start.3 = (bf16[128]{0:T(256)(128)(2,1)S(1)}, bf16[128]{0:T(256)(128)(2,1)S(1)}, u32[]{:S(2)}, u32[]{:S(2)}) collective-permute-start(bf16[128]{0:T(256)(128)(2,1)S(1)} %convert_element_type.56), channel_id=1, source_target_pairs={{0,63},{1,0},{2,1},{3,2},{4,3},{5,4},{6,5},{7,6},{8,7},{9,8},{10,9... | collective-permute-start | bytes 776 | tf_op jit(solution)/shard_map/ppermute | solution.py:14
  23.6 39.5 %collective-permute-start.1 = (bf16[128,1280]{1,0:T(8,128)(2,1)S(1)}, bf16[128,1280]{1,0:T(8,128)(2,1)S(1)}, u32[]{:S(2)}, u32[]{:S(2)}) collective-permute-start(bf16[128,1280]{1,0:T(8,128)(2,1)S(1)} %bitcast.119), channel_id=1, source_target_pairs={{0,63},{1,0},{2,1},{3,2},{4,3},{5,4},{6,5},{7,6},{8,7},{9,8},{10,9... | collective-permute-start | bytes 983048 | tf_op jit(solution)/shard_map/ppermute | solution.py:14
  26.1 37.2 %collective-permute-start = (bf16[128,1280]{1,0:T(8,128)(2,1)S(1)}, bf16[128,1280]{1,0:T(8,128)(2,1)}, u32[]{:S(2)}, u32[]{:S(2)}) collective-permute-start(bf16[128,1280]{1,0:T(8,128)(2,1)S(1)} %bitcast.120), channel_id=1, source_target_pairs={{0,1},{1,2},{2,3},{3,4},{4,5},{5,6},{6,7},{7,8},{8,9},{9,10},{10,1... | collective-permute-start | bytes 983048 | tf_op jit(solution)/shard_map/ppermute | solution.py:14
  28.1 36.6 %collective-permute-start.5 = (bf16[128,1280]{1,0:T(8,128)(2,1)S(1)}, bf16[128,1280]{1,0:T(8,128)(2,1)}, u32[]{:S(2)}, u32[]{:S(2)}) collective-permute-start(bf16[128,1280]{1,0:T(8,128)(2,1)S(1)} %bitcast.121), channel_id=1, source_target_pairs={{0,63},{1,0},{2,1},{3,2},{4,3},{5,4},{6,5},{7,6},{8,7},{9,8},{10,9... | collective-permute-start | bytes 983048 | tf_op jit(solution)/shard_map/ppermute | solution.py:14
  36.0 30.7 %collective-permute-start.4 = (bf16[128,1280]{1,0:T(8,128)(2,1)S(1)}, bf16[128,1280]{1,0:T(8,128)(2,1)}, u32[]{:S(2)}, u32[]{:S(2)}) collective-permute-start(bf16[128,1280]{1,0:T(8,128)(2,1)S(1)} %bitcast.122), channel_id=1, source_target_pairs={{0,1},{1,2},{2,3},{3,4},{4,5},{5,6},{6,7},{7,8},{8,9},{9,10},{10,1... | collective-permute-start | bytes 983048 | tf_op jit(solution)/shard_map/ppermute | solution.py:14
  46.5 10.9 %copy-start.9 = (bf16[1,128,1280]{2,1,0:T(8,128)(2,1)S(1)}, bf16[1,128,1280]{2,1,0:T(8,128)(2,1)}, u32[]{:S(2)}) copy-start(bf16[1,128,1280]{2,1,0:T(8,128)(2,1)} %param.8) | copy-start | bytes 983044
  47.3 15.4 %copy-start.22 = (s32[1,4,12]{2,1,0:T(4,128)S(1)}, s32[1,4,12]{2,1,0:T(4,128)}, u32[]{:S(2)}) copy-start(s32[1,4,12]{2,1,0:T(4,128)} %param.14) | copy-start | bytes 580
  47.3 24.0 %all-to-all-start.1 = ((bf16[8,2,10240]{2,1,0:T(2,128)(2,1)}), bf16[8,2,10240]{2,1,0:T(2,128)(2,1)S(1)}, u32[]{:S(2)}, u32[]{:S(2)}) async-start(bf16[8,2,10240]{2,1,0:T(2,128)(2,1)} %reshape.81), calls=%async_computation.1 | async-start | bytes 655360 | tf_op jit(solution)/shard_map/all_to_all | solution.py:51
  53.4 15.1 %copy-start.12 = (bf16[1,128,1280]{1,2,0:T(8,128)(2,1)}, bf16[1,128,1280]{1,2,0:T(8,128)(2,1)S(1)}, u32[]{:S(2)}) copy-start(bf16[1,128,1280]{1,2,0:T(8,128)(2,1)S(1)} %copy.68) | copy-start | bytes 983044
  53.4 9.1 %collective-permute-start.2 = (bf16[128]{0:T(256)(128)(2,1)S(1)}, bf16[128]{0:T(256)(128)(2,1)S(1)}, u32[]{:S(2)}, u32[]{:S(2)}) collective-permute-start(bf16[128]{0:T(256)(128)(2,1)S(1)} %convert_element_type.56), channel_id=1, source_target_pairs={{0,1},{1,2},{2,3},{3,4},{4,5},{5,6},{6,7},{7,8},{8,9},{9,10},{10,1... | collective-permute-start | bytes 776 | tf_op jit(solution)/shard_map/ppermute | solution.py:14
  57.6 11.6 %copy-start.7 = (bf16[1,128,1280]{1,2,0:T(8,128)(2,1)}, bf16[1,128,1280]{1,2,0:T(8,128)(2,1)S(1)}, u32[]{:S(2)}) copy-start(bf16[1,128,1280]{1,2,0:T(8,128)(2,1)S(1)} %copy.71) | copy-start | bytes 983044
  63.3 5.9 %copy-start.15 = (bf16[128,1280]{0,1:T(8,128)(2,1)}, bf16[128,1280]{0,1:T(8,128)(2,1)S(1)}, u32[]{:S(2)}) copy-start(bf16[128,1280]{0,1:T(8,128)(2,1)S(1)} %copy.69) | copy-start | bytes 983044
  64.6 4.6 copy-start.17
  92.0 4.0 copy-start.1
  108.4 317.4 %all-to-all-start = ((bf16[8,2,10240]{2,1,0:T(2,128)(2,1)}), bf16[8,2,10240]{2,1,0:T(2,128)(2,1)S(1)}, u32[]{:S(2)}, u32[]{:S(2)}) async-start(bf16[8,2,10240]{2,1,0:T(2,128)(2,1)} %reshape.79), calls=%async_computation | async-start | bytes 655360 | tf_op jit(solution)/shard_map/all_to_all | solution.py:53
  430.4 7.3 %copy-start.4 = (bf16[1,128,1280]{1,2,0:T(8,128)(2,1)S(1)}, bf16[1,128,1280]{1,2,0:T(8,128)(2,1)}, u32[]{:S(2)}) copy-start(bf16[1,128,1280]{1,2,0:T(8,128)(2,1)} %copy.102) | copy-start | bytes 983044
  430.4 7.3 %copy-start.5 = (bf16[8,128,160]{1,2,0:T(8,128)(2,1)S(1)}, bf16[8,128,160]{1,2,0:T(8,128)(2,1)}, u32[]{:S(2)}) copy-start(bf16[8,128,160]{1,2,0:T(8,128)(2,1)} %copy.101) | copy-start | bytes 983044
  432.2 5.6 %copy-start.14 = (bf16[1,128,1280]{1,2,0:T(8,128)(2,1)S(1)}, bf16[1,128,1280]{1,2,0:T(8,128)(2,1)}, u32[]{:S(2)}) copy-start(bf16[1,128,1280]{1,2,0:T(8,128)(2,1)} %copy.76) | copy-start | bytes 983044
  432.2 5.6 %copy-start.19 = (bf16[128,1280]{0,1:T(8,128)(2,1)S(1)}, bf16[128,1280]{0,1:T(8,128)(2,1)}, u32[]{:S(2)}) copy-start(bf16[128,1280]{0,1:T(8,128)(2,1)} %copy.77) | copy-start | bytes 983044
  432.2 5.7 %copy-start.20 = (bf16[128,1280]{0,1:T(8,128)(2,1)S(1)}, bf16[128,1280]{0,1:T(8,128)(2,1)}, u32[]{:S(2)}) copy-start(bf16[128,1280]{0,1:T(8,128)(2,1)} %copy.75) | copy-start | bytes 983044
  433.2 17.9 %collective-permute-start.8 = (bf16[128,8,160]{0,2,1:T(8,128)(2,1)}, bf16[128,8,160]{0,2,1:T(8,128)(2,1)}, u32[]{:S(2)}, u32[]{:S(2)}) collective-permute-start(bf16[128,8,160]{0,2,1:T(8,128)(2,1)} %get-tuple-element.20), channel_id=1, source_target_pairs={{0,63},{1,0},{2,1},{3,2},{4,3},{5,4},{6,5},{7,6},{8,7},{9,8},{10,9... | collective-permute-start | bytes 983048 | tf_op jit(solution)/shard_map/ppermute | solution.py:14
  435.3 16.4 %collective-permute-start.9 = (bf16[128,8,160]{0,2,1:T(8,128)(2,1)}, bf16[128,8,160]{0,2,1:T(8,128)(2,1)}, u32[]{:S(2)}, u32[]{:S(2)}) collective-permute-start(bf16[128,8,160]{0,2,1:T(8,128)(2,1)} %get-tuple-element.21), channel_id=1, source_target_pairs={{0,1},{1,2},{2,3},{3,4},{4,5},{5,6},{6,7},{7,8},{8,9},{9,10},{10,1... | collective-permute-start | bytes 983048 | tf_op jit(solution)/shard_map/ppermute | solution.py:14
  438.9 10.8 %copy-start.13 = (bf16[1,128,1280]{1,2,0:T(8,128)(2,1)S(1)}, bf16[1,128,1280]{1,2,0:T(8,128)(2,1)}, u32[]{:S(2)}) copy-start(bf16[1,128,1280]{1,2,0:T(8,128)(2,1)} %copy-done.12) | copy-start | bytes 983044
  438.9 10.8 %copy-start.16 = (bf16[128,1280]{0,1:T(8,128)(2,1)S(1)}, bf16[128,1280]{0,1:T(8,128)(2,1)}, u32[]{:S(2)}) copy-start(bf16[128,1280]{0,1:T(8,128)(2,1)} %copy-done.15) | copy-start | bytes 983044
  438.9 10.9 %copy-start.18 = (bf16[128,1280]{0,1:T(8,128)(2,1)S(1)}, bf16[128,1280]{0,1:T(8,128)(2,1)}, u32[]{:S(2)}) copy-start(bf16[128,1280]{0,1:T(8,128)(2,1)} %copy-done.17) | copy-start | bytes 983044
  440.2 13.9 %collective-permute-start.6 = (bf16[128,8,160]{0,2,1:T(8,128)(2,1)}, bf16[128,8,160]{0,2,1:T(8,128)(2,1)}, u32[]{:S(2)}, u32[]{:S(2)}) collective-permute-start(bf16[128,8,160]{0,2,1:T(8,128)(2,1)} %get-tuple-element.22), channel_id=1, source_target_pairs={{0,63},{1,0},{2,1},{3,2},{4,3},{5,4},{6,5},{7,6},{8,7},{9,8},{10,9... | collective-permute-start | bytes 983048 | tf_op jit(solution)/shard_map/ppermute | solution.py:14
  447.8 16.2 %collective-permute-start.7 = (bf16[128,8,160]{0,2,1:T(8,128)(2,1)S(1)}, bf16[128,8,160]{0,2,1:T(8,128)(2,1)}, u32[]{:S(2)}, u32[]{:S(2)}) collective-permute-start(bf16[128,8,160]{0,2,1:T(8,128)(2,1)S(1)} %get-tuple-element.23), channel_id=1, source_target_pairs={{0,1},{1,2},{2,3},{3,4},{4,5},{5,6},{6,7},{7,8},{8,9},{9,10},{10,1... | collective-permute-start | bytes 983048 | tf_op jit(solution)/shard_map/ppermute | solution.py:14
  (4 other events, 7.4 us)
Sparse Core Ops, SparseCore 0:
  10.7 81.2 all-gather.1
where the time goes:
time: 474 us; the launch traced here: 473 us
  blocking collectives  307 us (65%)
  starting transfers between devices  59.8 us (13%)
  waiting for transfers between devices  35.6 us (8%)
  local copies, waits for them, and re-layouts  26.6 us (6%)
  other arithmetic  18.1 us (4%)
  between operations  15.3 us (3%)
  matrix products  10.4 us (2%)
    psum x1, blocking collectives, local(): d_weight = lax.psum(weight_part, 'region').astype(jnp.bfloat16)  307 us
    ppermute x10, starting transfers between devices, from_behind(): lax.ppermute(value, axis, [(i, (i + by) % length) for i in range(length)])  43.7 us
    all_gather x1, waiting for transfers between devices, local(): gathered = lax.all_gather(grads, 'dp', axis=1, tiled=True)  20.1 us
    unnamed x62, local copies, waits for them, and re-layouts  16 us
    ppermute x10, waiting for transfers between devices, from_behind(): lax.ppermute(value, axis, [(i, (i + by) % length) for i in range(length)])  15.5 us
    unnamed x2, other arithmetic  12.4 us
    all_to_all x1, starting transfers between devices, local(): lax.all_to_all(attn_part.astype(jnp.bfloat16)[None], 'dp', split_axis=1,...  10.2 us
  transfers between devices with their start and end apart: 13, of which 4 were waited for; matrix products, arithmetic and copies ran while one was open for 5% of the time, Pallas kernels for 0%

commit v1 on v0

--- a/solution.py
+++ b/solution.py
@@ -47,7 +47,9 @@
     live_blocks = jnp.arange(BLK) < counts[0]
     live_rows = jnp.repeat(live_blocks, block_rows)
     grads = d_out * live_rows[None, :, None].astype(jnp.bfloat16)
-    gathered = lax.all_gather(grads, "dp", axis=1, tiled=True)
+    gathered = jnp.concatenate(
+        lax.all_to_all(jnp.stack([grads] * lax.axis_size("dp")), "dp", 0, 0), axis=1
+    )
     out_cols = lax.all_to_all(attn_out, "dp", split_axis=2, concat_axis=1, tiled=True)
     attn_part = jnp.einsum("td,hd->th", gathered[0], w_out, preferred_element_type=jnp.float32)
     d_attn = lax.all_to_all(

time: 474 us -> 479 us (1.011)
  the two profiles are of different devices: /device:TPU:2 before, /device:TPU:4 now
where the time goes in v1:
time: 479 us; the launch traced here: 478 us
  blocking collectives  313 us (65%)
  starting transfers between devices  59 us (12%)
  waiting for transfers between devices  47.4 us (10%)
  local copies, waits for them, and re-layouts  26.9 us (6%)
  other arithmetic  15.8 us (3%)
  matrix products  13.9 us (3%)
    psum x1, blocking collectives, local(): d_weight = lax.psum(weight_part, 'region').astype(jnp.bfloat16)  313 us
    ppermute x10, waiting for transfers between devices, from_behind(): lax.ppermute(value, axis, [(i, (i + by) % length) for i in range(length)])  39.5 us
    ppermute x10, starting transfers between devices, from_behind(): lax.ppermute(value, axis, [(i, (i + by) % length) for i in range(length)])  37.8 us
    unnamed x50, local copies, waits for them, and re-layouts  16.1 us
    unnamed x2, other arithmetic  11.5 us
  transfers between devices with their start and end apart: 13, of which 4 were waited for; matrix products, arithmetic and copies ran while one was open for 5% of the time, Pallas kernels for 0%

profile of v1, /device:TPU:4, one launch (start us, length us, event | category | flops | bytes accessed | tf_op | source)
XLA Modules:
  0.0 478.0 jit_solution(2722282103875781250)
XLA Ops:
  0.7 1.5 copy.83
  2.7 7.4 %reduce.5 = bf16[1280,128]{1,0:T(8,128)(2,1)S(1)} reduce(bf16[1280,1,128]{2,1,0:T(2,128)(2,1)S(1)} %bitcast.100, bf16[]{:T(256)} %broadcast.43), dimensions={1}, to_apply=%bitcast.82.reduce_sub_computation | reduce | bytes 655362
  10.9 9.2 %all-to-all-start.2 = ((bf16[8,2,10240]{2,1,0:T(2,128)(2,1)}), bf16[8,2,10240]{2,1,0:T(2,128)(2,1)S(1)}, u32[]{:S(2)}, u32[]{:S(2)}) async-start(bf16[8,2,10240]{2,1,0:T(2,128)(2,1)} %reshape.84), calls=%async_computation.2 | async-start | bytes 655360 | tf_op jit(solution)/shard_map/all_to_all | solution.py:53
  21.1 4.0 all-to-all-done.2
  25.1 2.8 stack.2
  27.9 7.2 %all-to-all-start = ((bf16[8,1,128,2560]{3,2,1,0:T(8,128)(2,1)}), bf16[8,1,128,2560]{3,2,1,0:T(8,128)(2,1)}, u32[]{:S(2)}, u32[]{:S(2)}) async-start(bf16[8,1,128,2560]{3,2,1,0:T(8,128)(2,1)} %stack.2), calls=%async_computation | async-start | bytes 10485760 | tf_op jit(solution)/shard_map/all_to_all | solution.py:51
  35.1 2.0 collective-permute-start.2
  37.2 3.9 collective-permute-start
  41.1 6.1 %collective-permute-start.1 = (bf16[128,1280]{1,0:T(8,128)(2,1)S(1)}, bf16[128,1280]{1,0:T(8,128)(2,1)}, u32[]{:S(2)}, u32[]{:S(2)}) collective-permute-start(bf16[128,1280]{1,0:T(8,128)(2,1)S(1)} %bitcast.114), channel_id=1, source_target_pairs={{0,63},{1,0},{2,1},{3,2},{4,3},{5,4},{6,5},{7,6},{8,7},{9,8},{10,9... | collective-permute-start | bytes 983048 | tf_op jit(solution)/shard_map/ppermute | solution.py:14
  47.2 1.9 collective-permute-start.4
  49.2 7.9 %collective-permute-start.5 = (bf16[128,1280]{1,0:T(8,128)(2,1)S(1)}, bf16[128,1280]{1,0:T(8,128)(2,1)S(1)}, u32[]{:S(2)}, u32[]{:S(2)}) collective-permute-start(bf16[128,1280]{1,0:T(8,128)(2,1)S(1)} %bitcast.116), channel_id=1, source_target_pairs={{0,63},{1,0},{2,1},{3,2},{4,3},{5,4},{6,5},{7,6},{8,7},{9,8},{10,9... | collective-permute-start | bytes 983048 | tf_op jit(solution)/shard_map/ppermute | solution.py:14
  57.3 2.1 collective-permute-start.3
  61.5 30.5 %collective-permute-done.3 = bf16[128]{0:T(256)(128)(2,1)S(1)} collective-permute-done((bf16[128]{0:T(256)(128)(2,1)S(1)}, bf16[128]{0:T(256)(128)(2,1)S(1)}, u32[]{:S(2)}, u32[]{:S(2)}) %collective-permute-start.3) | collective-permute-done | bytes 288 | tf_op jit(solution)/shard_map/ppermute | solution.py:14
  93.8 1.3 copy.69
  99.6 3.9 all-to-all-done
  103.5 4.3 fusion.7
  108.7 4.0 reduce.4
  112.7 1.6 reshape.82
  114.3 4.8 %all-to-all-start.1 = ((bf16[8,2,10240]{2,1,0:T(2,128)(2,1)}), bf16[8,2,10240]{2,1,0:T(2,128)(2,1)S(1)}, u32[]{:S(2)}, u32[]{:S(2)}) async-start(bf16[8,2,10240]{2,1,0:T(2,128)(2,1)} %reshape.82), calls=%async_computation.1 | async-start | bytes 655360 | tf_op jit(solution)/shard_map/all_to_all | solution.py:55
  119.1 3.5 convolution_bitcast_fusion
  122.6 313.3 %all-reduce.1 = bf16[160,2560]{1,0:T(8,128)(2,1)} all-reduce(f32[160,2560]{1,0:T(8,128)S(1)} %convolution_bitcast_fusion), channel_id=1, replica_groups=mesh['dp'=8,'region'=64] {'region'}, use_global_device_ids=true, to_apply=%region_2.3 | all-reduce | flops 409600 | bytes 2457600 | tf_op jit(solution)/shard_map/psum | solution.py:61
  435.9 2.1 reshape.83
  438.0 1.3 copy.104
  439.5 1.8 fusion.34
  442.3 1.9 collective-permute-start.8
  444.2 2.6 collective-permute-start.9
  449.0 2.0 multiply_convert_fusion
  452.3 7.4 %collective-permute-start.6 = (bf16[128,8,160]{0,2,1:T(8,128)(2,1)}, bf16[128,8,160]{0,2,1:T(8,128)(2,1)}, u32[]{:S(2)}, u32[]{:S(2)}) collective-permute-start(bf16[128,8,160]{0,2,1:T(8,128)(2,1)} %get-tuple-element.22), channel_id=1, source_target_pairs={{0,63},{1,0},{2,1},{3,2},{4,3},{5,4},{6,5},{7,6},{8,7},{9,8},{10,9... | collective-permute-start | bytes 983048 | tf_op jit(solution)/shard_map/ppermute | solution.py:14
  459.7 1.9 collective-permute-start.7
  462.8 1.9 copy.85
  464.7 1.4 fusion.18
  467.0 9.0 %collective-permute-done.7 = bf16[128,8,160]{0,2,1:T(8,128)(2,1)} collective-permute-done((bf16[128,8,160]{0,2,1:T(8,128)(2,1)S(1)}, bf16[128,8,160]{0,2,1:T(8,128)(2,1)}, u32[]{:S(2)}, u32[]{:S(2)}) %collective-permute-start.7) | collective-permute-done | bytes 327712 | tf_op jit(solution)/shard_map/ppermute | solution.py:14
  (82 shorter events, 19.7 us)
Async XLA Ops:
  0.6 102.9 %copy-start = (bf16[160,2560]{1,0:T(8,128)(2,1)S(1)}, bf16[160,2560]{1,0:T(8,128)(2,1)}, u32[]{:S(2)}) copy-start(bf16[160,2560]{1,0:T(8,128)(2,1)} %param.13) | copy-start | bytes 2457604
  0.6 20.3 %copy-start.6 = (bf16[1,128,2560]{2,1,0:T(8,128)(2,1)S(1)}, bf16[1,128,2560]{2,1,0:T(8,128)(2,1)}, u32[]{:S(2)}) copy-start(bf16[1,128,2560]{2,1,0:T(8,128)(2,1)} %param.12) | copy-start | bytes 1966084
  10.9 14.2 %all-to-all-start.2 = ((bf16[8,2,10240]{2,1,0:T(2,128)(2,1)}), bf16[8,2,10240]{2,1,0:T(2,128)(2,1)S(1)}, u32[]{:S(2)}, u32[]{:S(2)}) async-start(bf16[8,2,10240]{2,1,0:T(2,128)(2,1)} %reshape.84), calls=%async_computation.2 | async-start | bytes 655360 | tf_op jit(solution)/shard_map/all_to_all | solution.py:53
  27.9 9.3 %copy-start.8 = (bf16[1,128,1280]{2,1,0:T(8,128)(2,1)S(1)}, bf16[1,128,1280]{2,1,0:T(8,128)(2,1)}, u32[]{:S(2)}) copy-start(bf16[1,128,1280]{2,1,0:T(8,128)(2,1)} %param.9) | copy-start | bytes 983044
  27.9 19.3 %copy-start.9 = (bf16[1,128,1280]{2,1,0:T(8,128)(2,1)S(1)}, bf16[1,128,1280]{2,1,0:T(8,128)(2,1)}, u32[]{:S(2)}) copy-start(bf16[1,128,1280]{2,1,0:T(8,128)(2,1)} %param.10) | copy-start | bytes 983044
  27.9 31.5 %copy-start.3 = (bf16[1,128,1280]{2,1,0:T(8,128)(2,1)S(1)}, bf16[1,128,1280]{2,1,0:T(8,128)(2,1)}, u32[]{:S(2)}) copy-start(bf16[1,128,1280]{2,1,0:T(8,128)(2,1)} %param.11) | copy-start | bytes 983044
  27.9 75.6 %all-to-all-start = ((bf16[8,1,128,2560]{3,2,1,0:T(8,128)(2,1)}), bf16[8,1,128,2560]{3,2,1,0:T(8,128)(2,1)}, u32[]{:S(2)}, u32[]{:S(2)}) async-start(bf16[8,1,128,2560]{3,2,1,0:T(8,128)(2,1)} %stack.2), calls=%async_computation | async-start | bytes 10485760 | tf_op jit(solution)/shard_map/all_to_all | solution.py:51
  35.1 26.1 %copy-start.7 = (bf16[1,128,1280]{2,1,0:T(8,128)(2,1)S(1)}, bf16[1,128,1280]{2,1,0:T(8,128)(2,1)}, u32[]{:S(2)}) copy-start(bf16[1,128,1280]{2,1,0:T(8,128)(2,1)} %param.8) | copy-start | bytes 983044
  35.1 57.1 %copy-start.16 = (s32[1,4,12]{2,1,0:T(4,128)S(1)}, s32[1,4,12]{2,1,0:T(4,128)}, u32[]{:S(2)}) copy-start(s32[1,4,12]{2,1,0:T(4,128)} %param.14) | copy-start | bytes 580
  35.1 22.1 %collective-permute-start.2 = (bf16[128]{0:T(256)(128)(2,1)S(1)}, bf16[128]{0:T(256)(128)(2,1)S(1)}, u32[]{:S(2)}, u32[]{:S(2)}) collective-permute-start(bf16[128]{0:T(256)(128)(2,1)S(1)} %convert_element_type.56), channel_id=1, source_target_pairs={{0,1},{1,2},{2,3},{3,4},{4,5},{5,6},{6,7},{7,8},{8,9},{9,10},{10,1... | collective-permute-start | bytes 776 | tf_op jit(solution)/shard_map/ppermute | solution.py:14
  37.2 55.4 %collective-permute-start = (bf16[128,1280]{1,0:T(8,128)(2,1)S(1)}, bf16[128,1280]{1,0:T(8,128)(2,1)}, u32[]{:S(2)}, u32[]{:S(2)}) collective-permute-start(bf16[128,1280]{1,0:T(8,128)(2,1)S(1)} %bitcast.113), channel_id=1, source_target_pairs={{0,1},{1,2},{2,3},{3,4},{4,5},{5,6},{6,7},{7,8},{8,9},{9,10},{10,1... | collective-permute-start | bytes 983048 | tf_op jit(solution)/shard_map/ppermute | solution.py:14
  41.1 52.7 %collective-permute-start.1 = (bf16[128,1280]{1,0:T(8,128)(2,1)S(1)}, bf16[128,1280]{1,0:T(8,128)(2,1)}, u32[]{:S(2)}, u32[]{:S(2)}) collective-permute-start(bf16[128,1280]{1,0:T(8,128)(2,1)S(1)} %bitcast.114), channel_id=1, source_target_pairs={{0,63},{1,0},{2,1},{3,2},{4,3},{5,4},{6,5},{7,6},{8,7},{9,8},{10,9... | collective-permute-start | bytes 983048 | tf_op jit(solution)/shard_map/ppermute | solution.py:14
  47.2 47.9 %collective-permute-start.4 = (bf16[128,1280]{1,0:T(8,128)(2,1)S(1)}, bf16[128,1280]{1,0:T(8,128)(2,1)S(1)}, u32[]{:S(2)}, u32[]{:S(2)}) collective-permute-start(bf16[128,1280]{1,0:T(8,128)(2,1)S(1)} %bitcast.115), channel_id=1, source_target_pairs={{0,1},{1,2},{2,3},{3,4},{4,5},{5,6},{6,7},{7,8},{8,9},{9,10},{10,1... | collective-permute-start | bytes 983048 | tf_op jit(solution)/shard_map/ppermute | solution.py:14
  49.2 46.8 %collective-permute-start.5 = (bf16[128,1280]{1,0:T(8,128)(2,1)S(1)}, bf16[128,1280]{1,0:T(8,128)(2,1)S(1)}, u32[]{:S(2)}, u32[]{:S(2)}) collective-permute-start(bf16[128,1280]{1,0:T(8,128)(2,1)S(1)} %bitcast.116), channel_id=1, source_target_pairs={{0,63},{1,0},{2,1},{3,2},{4,3},{5,4},{6,5},{7,6},{8,7},{9,8},{10,9... | collective-permute-start | bytes 983048 | tf_op jit(solution)/shard_map/ppermute | solution.py:14
  57.2 39.7 %copy-start.10 = (bf16[1,128,1280]{1,2,0:T(8,128)(2,1)}, bf16[1,128,1280]{1,2,0:T(8,128)(2,1)S(1)}, u32[]{:S(2)}) copy-start(bf16[1,128,1280]{1,2,0:T(8,128)(2,1)S(1)} %copy.68) | copy-start | bytes 983044
  57.3 34.7 %collective-permute-start.3 = (bf16[128]{0:T(256)(128)(2,1)S(1)}, bf16[128]{0:T(256)(128)(2,1)S(1)}, u32[]{:S(2)}, u32[]{:S(2)}) collective-permute-start(bf16[128]{0:T(256)(128)(2,1)S(1)} %convert_element_type.56), channel_id=1, source_target_pairs={{0,63},{1,0},{2,1},{3,2},{4,3},{5,4},{6,5},{7,6},{8,7},{9,8},{10,9... | collective-permute-start | bytes 776 | tf_op jit(solution)/shard_map/ppermute | solution.py:14
  61.4 36.2 %copy-start.4 = (bf16[1,128,1280]{1,2,0:T(8,128)(2,1)}, bf16[1,128,1280]{1,2,0:T(8,128)(2,1)S(1)}, u32[]{:S(2)}) copy-start(bf16[1,128,1280]{1,2,0:T(8,128)(2,1)S(1)} %copy.71) | copy-start | bytes 983044
  93.8 3.9 copy-start.12
  95.1 2.6 copy-start.14
  97.6 1.1 copy-start.1
  114.3 321.6 %all-to-all-start.1 = ((bf16[8,2,10240]{2,1,0:T(2,128)(2,1)}), bf16[8,2,10240]{2,1,0:T(2,128)(2,1)S(1)}, u32[]{:S(2)}, u32[]{:S(2)}) async-start(bf16[8,2,10240]{2,1,0:T(2,128)(2,1)} %reshape.82), calls=%async_computation.1 | async-start | bytes 655360 | tf_op jit(solution)/shard_map/all_to_all | solution.py:55
  435.9 3.6 copy-start.2
  442.3 22.4 %collective-permute-start.8 = (bf16[128,8,160]{0,2,1:T(8,128)(2,1)}, bf16[128,8,160]{0,2,1:T(8,128)(2,1)}, u32[]{:S(2)}, u32[]{:S(2)}) collective-permute-start(bf16[128,8,160]{0,2,1:T(8,128)(2,1)} %get-tuple-element.20), channel_id=1, source_target_pairs={{0,63},{1,0},{2,1},{3,2},{4,3},{5,4},{6,5},{7,6},{8,7},{9,8},{10,9... | collective-permute-start | bytes 983048 | tf_op jit(solution)/shard_map/ppermute | solution.py:14
  444.2 20.5 %collective-permute-start.9 = (bf16[128,8,160]{0,2,1:T(8,128)(2,1)}, bf16[128,8,160]{0,2,1:T(8,128)(2,1)}, u32[]{:S(2)}, u32[]{:S(2)}) collective-permute-start(bf16[128,8,160]{0,2,1:T(8,128)(2,1)} %get-tuple-element.21), channel_id=1, source_target_pairs={{0,1},{1,2},{2,3},{3,4},{4,5},{5,6},{6,7},{7,8},{8,9},{9,10},{10,1... | collective-permute-start | bytes 983048 | tf_op jit(solution)/shard_map/ppermute | solution.py:14
  448.9 2.0 copy-start.5
  451.0 10.6 %copy-start.11 = (bf16[1,128,1280]{1,2,0:T(8,128)(2,1)S(1)}, bf16[1,128,1280]{1,2,0:T(8,128)(2,1)}, u32[]{:S(2)}) copy-start(bf16[1,128,1280]{1,2,0:T(8,128)(2,1)} %copy-done.10) | copy-start | bytes 983044
  451.0 10.6 %copy-start.13 = (bf16[128,1280]{0,1:T(8,128)(2,1)S(1)}, bf16[128,1280]{0,1:T(8,128)(2,1)}, u32[]{:S(2)}) copy-start(bf16[128,1280]{0,1:T(8,128)(2,1)} %copy-done.12) | copy-start | bytes 983044
  451.0 10.6 %copy-start.15 = (bf16[128,1280]{0,1:T(8,128)(2,1)S(1)}, bf16[128,1280]{0,1:T(8,128)(2,1)}, u32[]{:S(2)}) copy-start(bf16[128,1280]{0,1:T(8,128)(2,1)} %copy-done.14) | copy-start | bytes 983044
  452.3 14.7 %collective-permute-start.6 = (bf16[128,8,160]{0,2,1:T(8,128)(2,1)}, bf16[128,8,160]{0,2,1:T(8,128)(2,1)}, u32[]{:S(2)}, u32[]{:S(2)}) collective-permute-start(bf16[128,8,160]{0,2,1:T(8,128)(2,1)} %get-tuple-element.22), channel_id=1, source_target_pairs={{0,63},{1,0},{2,1},{3,2},{4,3},{5,4},{6,5},{7,6},{8,7},{9,8},{10,9... | collective-permute-start | bytes 983048 | tf_op jit(solution)/shard_map/ppermute | solution.py:14
  459.7 16.2 %collective-permute-start.7 = (bf16[128,8,160]{0,2,1:T(8,128)(2,1)S(1)}, bf16[128,8,160]{0,2,1:T(8,128)(2,1)}, u32[]{:S(2)}, u32[]{:S(2)}) collective-permute-start(bf16[128,8,160]{0,2,1:T(8,128)(2,1)S(1)} %get-tuple-element.23), channel_id=1, source_target_pairs={{0,1},{1,2},{2,3},{3,4},{4,5},{5,6},{6,7},{7,8},{8,9},{9,10},{10,1... | collective-permute-start | bytes 983048 | tf_op jit(solution)/shard_map/ppermute | solution.py:14
